TPU v7x, 1024 devices: a whole 4x8x16 slice. The times are simulated.
1024 devices in a mesh: pipe: 8 (over y_hi, x), expert: 32 (over z, core), dp: 4 (over y_lo).
Axes of the slice: x: 4, y: 8 (y_hi: 2, y_lo: 4; y = y_hi * 4 + y_lo), z: 16, core: 2. Of those that a mesh axis runs over, the one named last changes fastest.
Arguments:
- acts_fwd: bfloat16 [8, 512, 3584], P('pipe', ('expert', 'dp')), may hold values from -6 to 6
- ids_fwd: int32 [8, 512, 2], P('pipe', ('expert', 'dp')), may hold values from 0 to 3, all different within a row; in each aligned block of 4 rows (0 to 3, 4 to 7, ..., all dimensions but the last counted through in order) at most 3 rows name the same one
- scores_fwd: float32 [8, 512, 2], P('pipe', ('expert', 'dp')), may hold values from 0.05 to 0.95
- cot_bwd: bfloat16 [8, 512, 3584], P('pipe', ('expert', 'dp')), may hold values from -1.5 to 1.5
- ids_bwd: int32 [8, 512, 2], P('pipe', ('expert', 'dp')), may hold values from 0 to 3, all different within a row; in each aligned block of 4 rows (0 to 3, 4 to 7, ..., all dimensions but the last counted through in order) at most 3 rows name the same one
- scores_bwd: float32 [8, 512, 2], P('pipe', ('expert', 'dp')), may hold values from 0.05 to 0.95
- saved_out: bfloat16 [8, 512, 2, 3584], P('pipe', ('expert', 'dp')), may hold values from -1.5 to 1.5
- saved_pre: bfloat16 [8, 384, 2, 8192], P('pipe', 'dp', None, 'expert'), may hold values from -6 to 6
- w_gate: bfloat16 [8, 3584, 8192], P('pipe', None, 'expert'), may hold values from -0.09375 to 0.09375
- w_up: bfloat16 [8, 3584, 8192], P('pipe', None, 'expert'), may hold values from -0.09375 to 0.09375
- w_down: bfloat16 [8, 8192, 3584], P('pipe', 'expert'), may hold values from -0.125 to 0.125
Outputs:
- acts_sent: bfloat16 [8, 512, 3584], P('pipe', ('expert', 'dp'))
- grads_sent: bfloat16 [8, 512, 3584], P('pipe', ('expert', 'dp'))
- score_grads: float32 [8, 512, 2], P('pipe', ('expert', 'dp'))
- down_grad: float32 [8, 3584, 8192], P('pipe', 'dp', 'expert')
Inputs may be any that keep to these rules, and one draw needn't show every extreme that they name: `ids_fwd`: each row names 2 different experts. In the 4 rows of one device no expert is named more than 3 times, and in every draw some device names one expert exactly 3 times. `ids_bwd`: each row names 2 different experts. In the 4 rows of one device no expert is named more than 3 times, and in every draw some device names one expert exactly 3 times.
All inputs are finite; a program needn't handle non-finite values.
Results may differ from a plain program's by a relative error of at most 0.0059.
Values may be sent and summed in bfloat16 or wider, within the bound.
A program may use at most 32 MiB of HBM per device.

v0:
```python
import jax
import jax.numpy as jnp
from jax import lax
from jax.sharding import PartitionSpec as P

FE = 2048


def shifted(block, axis, distance):
    devices = range(lax.axis_size(axis))
    route = [(i - distance, i) for i in devices if i - distance in devices]
    return lax.ppermute(block, axis, route)


def mix_weights(scores):
    return 2.5 * scores / jnp.sum(scores, axis=-1, keepdims=True)


def score_gradient(scores, dots):
    score_total = jnp.sum(scores, axis=-1, keepdims=True)
    return 2.5 / score_total * (dots - jnp.sum(dots * scores, axis=-1, keepdims=True) / score_total)


def routing_slots(expert_ids):
    flat_ids = expert_ids.reshape(-1)
    pair_count = flat_ids.shape[0]
    same_expert = flat_ids[:, None] == flat_ids[None, :]
    earlier = lax.broadcasted_iota(jnp.int32, (pair_count, pair_count), 1) < lax.broadcasted_iota(
        jnp.int32, (pair_count, pair_count), 0
    )
    return jnp.sum(same_expert & earlier, axis=1).reshape(expert_ids.shape)


def dispatch_matrix(expert_ids, slot_ids, values, expert_count, capacity):
    slot_total = expert_count * capacity
    target = lax.broadcasted_iota(jnp.int32, (slot_total, 1, 1), 0)
    matched = (target // capacity == expert_ids[None]) & (target % capacity == slot_ids[None])
    return jnp.sum(jnp.where(matched, values[None], 0.0), axis=2)


def highest_dot(left, right):
    return jnp.dot(left, right, precision=lax.Precision.HIGHEST, preferred_element_type=jnp.float32)


def forward_part(slot_rows, gate_slice, up_slice, down_slice):
    gate_pre = jnp.dot(slot_rows, gate_slice, preferred_element_type=jnp.float32)
    up_pre = jnp.dot(slot_rows, up_slice, preferred_element_type=jnp.float32)
    hidden = (gate_pre * jax.nn.sigmoid(gate_pre) * up_pre).astype(jnp.bfloat16)
    return jnp.dot(hidden, down_slice, preferred_element_type=jnp.float32)


def backward_part(slot_rows, pre_rows, gate_slice, up_slice, down_slice):
    contract_last = (((1,), (1,)), ((), ()))
    grad_hidden = lax.dot_general(
        slot_rows, down_slice, contract_last, preferred_element_type=jnp.float32
    )
    gate_pre = pre_rows[:, 0].astype(jnp.float32)
    up_pre = pre_rows[:, 1].astype(jnp.float32)
    sigmoid_gate = jax.nn.sigmoid(gate_pre)
    grad_gate = (
        grad_hidden * up_pre * sigmoid_gate * (1.0 + gate_pre * (1.0 - sigmoid_gate))
    ).astype(jnp.bfloat16)
    grad_up = (grad_hidden * gate_pre * sigmoid_gate).astype(jnp.bfloat16)
    hidden = (gate_pre * sigmoid_gate * up_pre).astype(jnp.bfloat16)
    partial_value = lax.dot_general(
        grad_gate, gate_slice, contract_last, preferred_element_type=jnp.float32
    )
    partial_value = partial_value + lax.dot_general(
        grad_up, up_slice, contract_last, preferred_element_type=jnp.float32
    )
    return (partial_value, hidden)


def pass_section(section_block):
    return shifted(section_block, "pipe", -1)


def shards(
    acts_fwd,
    ids_fwd,
    scores_fwd,
    cot_bwd,
    ids_bwd,
    scores_bwd,
    saved_out,
    saved_pre,
    w_gate,
    w_up,
    w_down,
):
    n_expert = lax.axis_size("expert")
    model_width = acts_fwd.shape[2]
    units = w_gate.shape[2]
    group = FE // units
    expert_count = n_expert // group
    capacity = saved_pre.shape[1] // n_expert
    gate_slice = w_gate[0]
    up_slice = w_up[0]
    down_slice = w_down[0]
    pre_rows = saved_pre[0]
    acts32 = acts_fwd[0].astype(jnp.float32)
    cot32 = cot_bwd[0].astype(jnp.float32)
    fwd_ids = ids_fwd[0]
    bwd_ids = ids_bwd[0]
    fwd_weights = mix_weights(scores_fwd[0])
    bwd_weights = mix_weights(scores_bwd[0])
    fwd_slots = routing_slots(fwd_ids)
    bwd_slots = routing_slots(bwd_ids)
    unit_weights = jnp.ones_like(fwd_weights)
    fwd_send_map = dispatch_matrix(fwd_ids, fwd_slots, unit_weights, expert_count, capacity)
    fwd_back_map = dispatch_matrix(fwd_ids, fwd_slots, fwd_weights, expert_count, capacity)
    bwd_send_map = dispatch_matrix(bwd_ids, bwd_slots, bwd_weights, expert_count, capacity)
    bwd_back_map = dispatch_matrix(bwd_ids, bwd_slots, unit_weights, expert_count, capacity)

    def route_rows(send_map, rows32):
        packed = (
            highest_dot(send_map, rows32)
            .astype(jnp.bfloat16)
            .reshape(expert_count, capacity, model_width)
        )
        return jnp.repeat(packed, group, axis=0)[None]

    fwd_buffer = route_rows(fwd_send_map, acts32)
    bwd_buffer = route_rows(bwd_send_map, cot32)

    def expert_round(buffer, round_kinds):
        arrived = lax.all_to_all(buffer, "expert", split_axis=1, concat_axis=1, tiled=True)
        partials = []
        down_inputs = None
        for member, round_kind in enumerate(round_kinds):
            slot_rows = arrived[member].reshape(-1, model_width)
            if round_kind == "forward":
                partial_value = forward_part(slot_rows, gate_slice, up_slice, down_slice)
            else:
                partial_value, hidden = backward_part(
                    slot_rows, pre_rows, gate_slice, up_slice, down_slice
                )
                down_inputs = (slot_rows, hidden)
            partials.append(
                partial_value.astype(jnp.bfloat16).reshape(n_expert, capacity, model_width)
            )
        returned = lax.all_to_all(
            jnp.stack(partials, axis=0), "expert", split_axis=1, concat_axis=1, tiled=True
        )
        return (returned, down_inputs)

    def finish_rows(back_map, returned_rows, start_rows):
        grouped = returned_rows.astype(jnp.float32).reshape(
            expert_count, group, capacity, model_width
        )
        back_rows = jnp.sum(grouped, axis=1).reshape(expert_count * capacity, model_width)
        mixed = lax.dot_general(
            back_map,
            back_rows,
            (((0,), (0,)), ((), ())),
            precision=lax.Precision.HIGHEST,
            preferred_element_type=jnp.float32,
        )
        return (start_rows + mixed).astype(jnp.bfloat16)

    returned_fwd, _ = expert_round(fwd_buffer, ("forward",))
    acts_sent = pass_section(finish_rows(fwd_back_map, returned_fwd[0], acts32)[None])[0]
    returned_bwd, down_inputs = expert_round(bwd_buffer, ("backward",))
    grads_sent = pass_section(finish_rows(bwd_back_map, returned_bwd[0], cot32)[None])[0]
    cot_rows, hidden_rows = down_inputs
    down_grad = lax.psum_scatter(
        lax.dot_general(
            cot_rows, hidden_rows, (((0,), (0,)), ((), ())), preferred_element_type=jnp.float32
        ),
        "dp",
        scatter_dimension=0,
        tiled=True,
    )
    dots = jnp.einsum("tkd,td->tk", saved_out[0], cot_bwd[0], preferred_element_type=jnp.float32)
    score_grads = score_gradient(scores_bwd[0], dots)
    return (acts_sent[None], grads_sent[None], score_grads[None], down_grad[None])


def solution(mesh):
    in_specs = (
        P("pipe", ("expert", "dp"), None),
        P("pipe", ("expert", "dp"), None),
        P("pipe", ("expert", "dp"), None),
        P("pipe", ("expert", "dp"), None),
        P("pipe", ("expert", "dp"), None),
        P("pipe", ("expert", "dp"), None),
        P("pipe", ("expert", "dp"), None, None),
        P("pipe", "dp", None, "expert"),
        P("pipe", None, "expert"),
        P("pipe", None, "expert"),
        P("pipe", "expert", None),
    )
    out_specs = (
        P("pipe", ("expert", "dp"), None),
        P("pipe", ("expert", "dp"), None),
        P("pipe", ("expert", "dp"), None),
        P("pipe", "dp", "expert"),
    )
    return jax.shard_map(shards, mesh=mesh, in_specs=in_specs, out_specs=out_specs, check_vma=False)
```

profile of v0, /device:TPU:7, one launch (start us, length us, event | category | flops | bytes accessed | tf_op | source)
XLA Modules:
  0.0 270.8 jit_solution(16574929017989909234)
XLA Ops:
  7.2 0.9 copy.38
  12.6 0.8 compare_and_fusion
  13.4 1.1 convolution_convert_fusion.1
  14.6 1.2 broadcast_in_dim.64
  15.7 19.6 %all-to-all-start.2 = ((bf16[1,32,3,3584]{3,2,0,1:T(4,128)(2,1)}), bf16[1,32,3,3584]{3,2,0,1:T(4,128)(2,1)S(1)}, u32[]{:S(2)}, u32[]{:S(2)}) async-start(bf16[1,32,3,3584]{3,2,0,1:T(4,128)(2,1)} %bitcast.127), calls=%async_computation.2 | async-start | bytes 1835008 | tf_op jit(solution)/shard_map/all_to_all | solution.py:127
  35.7 49.7 %all-to-all-done.2 = bf16[1,32,3,3584]{3,2,0,1:T(4,128)(2,1)S(1)} async-done(((bf16[1,32,3,3584]{3,2,0,1:T(4,128)(2,1)}), bf16[1,32,3,3584]{3,2,0,1:T(4,128)(2,1)S(1)}, u32[]{:S(2)}, u32[]{:S(2)}) %all-to-all-start.2) | async-done | bytes 688160 | tf_op jit(solution)/shard_map/all_to_all | solution.py:127
  85.5 1.2 broadcast_in_dim.60
  86.7 4.1 %all-to-all-start = ((bf16[1,32,3,3584]{3,2,0,1:T(4,128)(2,1)}), bf16[1,32,3,3584]{3,2,0,1:T(4,128)(2,1)S(1)}, u32[]{:S(2)}, u32[]{:S(2)}) async-start(bf16[1,32,3,3584]{3,2,0,1:T(4,128)(2,1)} %bitcast.126), calls=%async_computation | async-start | bytes 1835008 | tf_op jit(solution)/shard_map/all_to_all | solution.py:127
  90.9 1.6 reshape_squeeze.7
  92.5 2.5 fusion.50
  95.0 2.3 fusion.5
  98.7 1.2 stack_reshape.7
  99.9 41.1 %all-to-all-done = bf16[1,32,3,3584]{3,2,0,1:T(4,128)(2,1)S(1)} async-done(((bf16[1,32,3,3584]{3,2,0,1:T(4,128)(2,1)}), bf16[1,32,3,3584]{3,2,0,1:T(4,128)(2,1)S(1)}, u32[]{:S(2)}, u32[]{:S(2)}) %all-to-all-start) | async-done | bytes 688160 | tf_op jit(solution)/shard_map/all_to_all | solution.py:127
  141.0 5.2 %all-to-all-start.3 = ((bf16[1,32,3,3584]{3,2,0,1:T(4,128)(2,1)}), bf16[1,32,3,3584]{3,2,0,1:T(4,128)(2,1)}, u32[]{:S(2)}, u32[]{:S(2)}) async-start(bf16[1,32,3,3584]{3,2,0,1:T(4,128)(2,1)} %bitcast.124), calls=%async_computation.3 | async-start | bytes 1835008 | tf_op jit(solution)/shard_map/all_to_all | solution.py:142
  146.9 1.9 fusion.13
  148.8 2.7 convolution_convert_fusion
  151.5 1.2 stack_reshape.6
  152.7 43.9 %all-to-all-done.3 = bf16[1,32,3,3584]{3,2,0,1:T(4,128)(2,1)} async-done(((bf16[1,32,3,3584]{3,2,0,1:T(4,128)(2,1)}), bf16[1,32,3,3584]{3,2,0,1:T(4,128)(2,1)}, u32[]{:S(2)}, u32[]{:S(2)}) %all-to-all-start.3) | async-done | bytes 688160 | tf_op jit(solution)/shard_map/all_to_all | solution.py:142
  196.5 4.5 %all-to-all-start.1 = ((bf16[1,32,3,3584]{3,2,0,1:T(4,128)(2,1)}), bf16[1,32,3,3584]{3,2,0,1:T(4,128)(2,1)S(1)}, u32[]{:S(2)}, u32[]{:S(2)}) async-start(bf16[1,32,3,3584]{3,2,0,1:T(4,128)(2,1)} %bitcast.7), calls=%async_computation.1 | async-start | bytes 1835008 | tf_op jit(solution)/shard_map/all_to_all | solution.py:142
  201.5 1.6 convert_reduce_fusion
  203.4 2.5 collective-permute-start.1
  205.9 45.4 %all-to-all-done.1 = bf16[1,32,3,3584]{3,2,0,1:T(4,128)(2,1)S(1)} async-done(((bf16[1,32,3,3584]{3,2,0,1:T(4,128)(2,1)}), bf16[1,32,3,3584]{3,2,0,1:T(4,128)(2,1)S(1)}, u32[]{:S(2)}, u32[]{:S(2)}) %all-to-all-start.1) | async-done | bytes 688160 | tf_op jit(solution)/shard_map/all_to_all | solution.py:142
  252.1 2.5 collective-permute-start
  255.1 7.6 %collective-permute-done = bf16[1,4,3584]{2,1,0:T(4,128)(2,1)S(1)} collective-permute-done((bf16[1,4,3584]{2,1,0:T(4,128)(2,1)S(1)}, bf16[1,4,3584]{2,1,0:T(4,128)(2,1)S(1)}, u32[]{:S(2)}, u32[]{:S(2)}) %collective-permute-start) | collective-permute-done | bytes 28704 | tf_op jit(solution)/shard_map/ppermute | solution.py:12
  (57 shorter events, 10.3 us)
Async XLA Ops:
  7.2 90.9 %copy-start = (bf16[1,3584,256]{2,1,0:T(8,128)(2,1)S(1)}, bf16[1,3584,256]{2,1,0:T(8,128)(2,1)}, u32[]{:S(2)}) copy-start(bf16[1,3584,256]{2,1,0:T(8,128)(2,1)} %param.20) | copy-start | bytes 5505028
  7.2 28.2 %copy-start.4 = (bf16[1,4,3584]{2,1,0:T(4,128)(2,1)S(1)}, bf16[1,4,3584]{2,1,0:T(4,128)(2,1)}, u32[]{:S(2)}) copy-start(bf16[1,4,3584]{2,1,0:T(4,128)(2,1)} %param.11) | copy-start | bytes 86020
  15.7 69.7 %all-to-all-start.2 = ((bf16[1,32,3,3584]{3,2,0,1:T(4,128)(2,1)}), bf16[1,32,3,3584]{3,2,0,1:T(4,128)(2,1)S(1)}, u32[]{:S(2)}, u32[]{:S(2)}) async-start(bf16[1,32,3,3584]{3,2,0,1:T(4,128)(2,1)} %bitcast.127), calls=%async_computation.2 | async-start | bytes 1835008 | tf_op jit(solution)/shard_map/all_to_all | solution.py:127
  35.3 55.5 %copy-start.6 = (bf16[1,96,2,256]{3,2,1,0:T(2,128)(2,1)S(1)}, bf16[1,96,2,256]{3,2,1,0:T(2,128)(2,1)}, u32[]{:S(2)}) copy-start(bf16[1,96,2,256]{3,2,1,0:T(2,128)(2,1)} %param.18) | copy-start | bytes 294916
  85.5 1.2 copy-start.2
  86.7 54.3 %all-to-all-start = ((bf16[1,32,3,3584]{3,2,0,1:T(4,128)(2,1)}), bf16[1,32,3,3584]{3,2,0,1:T(4,128)(2,1)S(1)}, u32[]{:S(2)}, u32[]{:S(2)}) async-start(bf16[1,32,3,3584]{3,2,0,1:T(4,128)(2,1)} %bitcast.126), calls=%async_computation | async-start | bytes 1835008 | tf_op jit(solution)/shard_map/all_to_all | solution.py:127
  90.8 171.9 %reduce-scatter.2.cloned.1.call-start = ((), (), s32[]{:S(2)}) async-start(), calls=%async_computation.5 | async-start | bytes 4587520 | tf_op jit(solution)/shard_map/reduce_scatter | solution.py:166
  95.0 2.3 copy-start.1
  141.0 55.5 %all-to-all-start.3 = ((bf16[1,32,3,3584]{3,2,0,1:T(4,128)(2,1)}), bf16[1,32,3,3584]{3,2,0,1:T(4,128)(2,1)}, u32[]{:S(2)}, u32[]{:S(2)}) async-start(bf16[1,32,3,3584]{3,2,0,1:T(4,128)(2,1)} %bitcast.124), calls=%async_computation.3 | async-start | bytes 1835008 | tf_op jit(solution)/shard_map/all_to_all | solution.py:142
  151.5 49.6 %copy-start.3 = (bf16[1,4,3584]{2,1,0:T(4,128)(2,1)S(1)}, bf16[1,4,3584]{2,1,0:T(4,128)(2,1)}, u32[]{:S(2)}) copy-start(bf16[1,4,3584]{2,1,0:T(4,128)(2,1)} %param.14) | copy-start | bytes 86020
  151.5 49.6 %copy-start.8 = (bf16[1,4,2,3584]{3,2,1,0:T(2,128)(2,1)S(1)}, bf16[1,4,2,3584]{3,2,1,0:T(2,128)(2,1)}, u32[]{:S(2)}) copy-start(bf16[1,4,2,3584]{3,2,1,0:T(2,128)(2,1)} %param.17) | copy-start | bytes 172036
  151.5 49.9 %copy-start.7 = (f32[1,4,2]{1,2,0:T(2,128)S(1)}, f32[1,4,2]{1,2,0:T(2,128)}, u32[]{:S(2)}) copy-start(f32[1,4,2]{1,2,0:T(2,128)} %param.16) | copy-start | bytes 100
  196.5 54.8 %all-to-all-start.1 = ((bf16[1,32,3,3584]{3,2,0,1:T(4,128)(2,1)}), bf16[1,32,3,3584]{3,2,0,1:T(4,128)(2,1)S(1)}, u32[]{:S(2)}, u32[]{:S(2)}) async-start(bf16[1,32,3,3584]{3,2,0,1:T(4,128)(2,1)} %bitcast.7), calls=%async_computation.1 | async-start | bytes 1835008 | tf_op jit(solution)/shard_map/all_to_all | solution.py:142
  201.3 50.5 %copy-start.5 = (bf16[1,4,3584]{2,1,0:T(4,128)(2,1)S(1)}, bf16[1,4,3584]{2,1,0:T(4,128)(2,1)}, u32[]{:S(2)}) copy-start(bf16[1,4,3584]{2,1,0:T(4,128)(2,1)} %param.11) | copy-start | bytes 86020
  203.4 51.7 %collective-permute-start.1 = (bf16[1,4,3584]{2,1,0:T(4,128)(2,1)S(1)}, bf16[1,4,3584]{2,1,0:T(4,128)(2,1)S(1)}, u32[]{:S(2)}, u32[]{:S(2)}) collective-permute-start(bf16[1,4,3584]{2,1,0:T(4,128)(2,1)S(1)} %fusion.3), channel_id=1, source_target_pairs={{128,0},{256,128},{384,256},{512,384},{640,512},{768,640},{896,768... | collective-permute-start | bytes 86024 | tf_op jit(solution)/shard_map/ppermute | solution.py:12
  252.1 10.6 %collective-permute-start = (bf16[1,4,3584]{2,1,0:T(4,128)(2,1)S(1)}, bf16[1,4,3584]{2,1,0:T(4,128)(2,1)S(1)}, u32[]{:S(2)}, u32[]{:S(2)}) collective-permute-start(bf16[1,4,3584]{2,1,0:T(4,128)(2,1)S(1)} %fusion.4), channel_id=1, source_target_pairs={{128,0},{256,128},{384,256},{512,384},{640,512},{768,640},{896,768... | collective-permute-start | bytes 86024 | tf_op jit(solution)/shard_map/ppermute | solution.py:12
Sparse Core Ops, SparseCore 0:
  95.6 81.7 reduce-scatter.1
where the time goes:
time: 273 us; the launch traced here: 271 us
  waiting for transfers between devices  188 us (69%)
  starting transfers between devices  38.4 us (14%)
  between operations  14.3 us (5%)
  matrix products  12.9 us (5%)
  local copies, waits for them, and re-layouts  10.9 us (4%)
  other arithmetic  6.65 us (2%)
    all_to_all x2, waiting for transfers between devices, expert_round(): lax.all_to_all(buffer, 'expert', split_axis=1, concat_axis=1, tiled=True)  90.8 us
    all_to_all x2, waiting for transfers between devices, expert_round(): lax.all_to_all(jnp.stack(partials, axis=0), 'expert', split_axis=1, conca...  89.3 us
    all_to_all x2, starting transfers between devices, expert_round(): lax.all_to_all(buffer, 'expert', split_axis=1, concat_axis=1, tiled=True)  23.7 us
    all_to_all x2, starting transfers between devices, expert_round(): lax.all_to_all(jnp.stack(partials, axis=0), 'expert', split_axis=1, conca...  9.73 us
    ppermute x2, waiting for transfers between devices, shifted(): return lax.ppermute(block, axis, route)  7.6 us
  transfers between devices with their start and end apart: 7, of which 5 were waited for; matrix products, arithmetic and copies ran while one was open for 7% of the time, Pallas kernels for 0%

commit v1 on v0

v1 whole, which is shorter than its diff:
```python
import functools

import jax
import jax.numpy as jnp
from jax import lax
from jax.experimental import pallas as pl
from jax.experimental.pallas import tpu as pltpu
from jax.sharding import PartitionSpec as P

FE = 2048
PIECES = 4
MESH = pl.DeviceIdType.MESH


def score_gradient(scores, dots):
    score_total = jnp.sum(scores, axis=-1, keepdims=True)
    return 2.5 / score_total * (dots - jnp.sum(dots * scores, axis=-1, keepdims=True) / score_total)


def column(row):
    n = row.shape[1]
    i = lax.broadcasted_iota(jnp.int32, (n, n), 0)
    j = lax.broadcasted_iota(jnp.int32, (n, n), 1)
    return jnp.sum(jnp.where(i == j, jnp.broadcast_to(row, (n, n)), 0.0), axis=1, keepdims=True)


def routing_rows(ids_t, scores_t, with_slots):
    ids = ids_t.astype(jnp.float32)
    weights = 2.5 * scores_t / jnp.sum(scores_t, axis=0, keepdims=True)
    tokens = ids.shape[1]
    lane = lax.broadcasted_iota(jnp.int32, (tokens, 128), 1).astype(jnp.float32)
    coefficient = jnp.zeros((tokens, 128), jnp.float32)
    hit = jnp.zeros((tokens, 128), jnp.float32)
    for k in range(2):
        expert = column(ids[k : k + 1])
        coefficient = coefficient + jnp.where(expert == lane, column(weights[k : k + 1]), 0.0)
        hit = hit + jnp.where(expert + 8.0 == lane, 1.0, 0.0)
    slots = jnp.full((tokens, 128), -1.0, jnp.float32)
    if with_slots:
        running = jnp.zeros((1, 128), jnp.float32)
        before = []
        for t in range(tokens):
            before.append(running)
            running = running + hit[t : t + 1]
        slots = jnp.where(hit > 0.0, jnp.concatenate(before, axis=0), -1.0)
    return jnp.where(lane < 8.0, coefficient, slots)


def dot(a, b):
    return jnp.dot(a, b, preferred_element_type=jnp.float32)


def dot_nt(a, b):
    return lax.dot_general(a, b, (((1,), (1,)), ((), ())), preferred_element_type=jnp.float32)


def dot_tn(a, b):
    return lax.dot_general(a, b, (((0,), (0,)), ((), ())), preferred_element_type=jnp.float32)


def kernel(
    n_pipe, n_dev, n_dp, group,
    acts_ref, cot_ref, ids_fwd_ref, scores_fwd_ref, ids_bwd_ref, scores_bwd_ref, pre_ref,
    wg_hbm, wu_hbm, wd_hbm,
    acts_out, grads_out, down_out,
    x, meta, wg, wu, wd, gate_acc, up_acc, gh_acc, placer, hid, sc, sc_send,
    sib_send, sib_recv, own, rs_send, rs_recv, fin_send, fin_recv,
    w_sem, ag_recv, ag_ring, ag_sib, hid_s, hid_r, sc_s, sc_r,
    sib_s, sib_r, rs_s, rs_r, fin_s, fin_r,
):
    n_chip = n_dev // 2
    half = n_chip // 2
    pipe = lax.axis_index("pipe")
    me = lax.axis_index("expert")
    mine_dp = lax.axis_index("dp")
    z, core = lax.div(me, 2), lax.rem(me, 2)
    sib = z * 2 + 1 - core
    right = lax.rem(z + 1, n_chip) * 2 + core
    left = lax.rem(z + n_chip - 1, n_chip) * 2 + core
    before, after = lax.rem(pipe + n_pipe - 1, n_pipe), lax.rem(pipe + 1, n_pipe)
    expert = lax.div(me, group)
    rows = n_dev * 8
    width = x.shape[3]
    slots = pre_ref.shape[1]
    cap = slots // n_dev

    def remote(src, dst, send_sem, recv_sem, **where):
        return pltpu.make_async_remote_copy(
            src_ref=src, dst_ref=dst, send_sem=send_sem, recv_sem=recv_sem,
            device_id=where, device_id_type=MESH,
        )

    barrier = pltpu.get_barrier_semaphore()
    peers = [dict(expert=right), dict(expert=left), dict(expert=sib)]
    peers += [dict(dp=lax.rem(mine_dp + r, n_dp)) for r in range(1, n_dp)]
    peers += [dict(pipe=p, expert=d) for p in (before, after) for d in (me, sib)]
    for peer in peers:
        pl.semaphore_signal(barrier, inc=1, device_id=peer, device_id_type=MESH)

    loads = []
    for q in range(PIECES):
        loads.append((
            pltpu.make_async_copy(wg_hbm.at[q], wg.at[q], w_sem.at[0, q]),
            pltpu.make_async_copy(wu_hbm.at[q], wu.at[q], w_sem.at[1, q]),
            pltpu.make_async_copy(wd_hbm.at[:, pl.ds(q * width, width)], wd.at[q], w_sem.at[2, q]),
        ))
        for load in loads[-1]:
            load.start()

    for q in range(PIECES):
        part = pl.ds(q * width, width)
        x[q, me] = jnp.concatenate(
            [acts_ref[:, part].astype(jnp.float32), cot_ref[:, part].astype(jnp.float32)], axis=0
        ).astype(jnp.bfloat16)
    meta[me] = jnp.concatenate(
        [
            routing_rows(ids_fwd_ref[...], scores_fwd_ref[...], False),
            routing_rows(ids_bwd_ref[...], scores_bwd_ref[...], True),
        ],
        axis=0,
    )
    gate_pre = pre_ref[0].astype(jnp.float32)
    up_pre = pre_ref[1].astype(jnp.float32)
    hid[n_dp - 1] = (gate_pre * jax.nn.sigmoid(gate_pre) * up_pre).astype(jnp.bfloat16)

    pl.semaphore_wait(barrier, len(peers))

    def block(q, d):
        return meta.at[d] if q == PIECES else x.at[q, d]

    order = (PIECES,) + tuple(range(PIECES))

    def hop(q, d, to, sem):
        return remote(block(q, d), block(q, d), sem, ag_recv.at[q, d], expert=to)

    def gather_wait(q, d):
        hop(q, d, sib, ag_sib.at[q, 0]).wait_recv()

    def gather_step(s, forward_plus, forward_minus, minus):
        plus_d = lax.rem(z + n_chip - s, n_chip) * 2 + core
        minus_d = lax.rem(z + s, n_chip) * 2 + core
        for q in order:
            gather_wait(q, plus_d)
            if forward_plus:
                hop(q, plus_d, right, ag_ring.at[q, 0, s]).start()
            hop(q, plus_d, sib, ag_sib.at[q, s]).start()
            if minus:
                gather_wait(q, minus_d)
                if forward_minus:
                    hop(q, minus_d, left, ag_ring.at[q, 1, s]).start()
                hop(q, minus_d, sib, ag_sib.at[q, n_chip - s]).start()

    for q in order:
        hop(q, me, right, ag_ring.at[q, 0, 0]).start()
        hop(q, me, left, ag_ring.at[q, 1, 0]).start()
        hop(q, me, sib, ag_sib.at[q, 0]).start()
    hid_copies = []
    for r in range(1, n_dp):
        hid_copies.append(remote(
            hid.at[n_dp - 1], hid.at[r - 1], hid_s.at[r - 1], hid_r.at[r - 1],
            dp=lax.rem(mine_dp + r, n_dp),
        ))
        hid_copies[-1].start()

    def gather_body(s, carry):
        gather_step(s, True, True, True)
        return carry

    lax.fori_loop(1, half - 1, gather_body, 0)
    gather_step(half - 1, True, False, True)
    gather_step(half, False, False, False)

    def sibling_wait(q):
        def body(i, carry):
            gather_wait(q, i * 2 + 1 - core)
            return carry

        lax.fori_loop(0, n_chip, body, 0)

    sibling_wait(PIECES)
    table = meta[...].reshape(rows, 128)
    lane = lax.broadcasted_iota(jnp.int32, (rows, 128), 1)
    coefficient = jnp.sum(jnp.where(lane == expert, table, 0.0), axis=1, keepdims=True)
    slot = jnp.sum(jnp.where(lane == expert + 8, table, 0.0), axis=1, keepdims=True)
    row = lax.broadcasted_iota(jnp.int32, (rows, 1), 0)
    forward_row = (row & 7) < 4
    target = jnp.where(slot < 0.0, -1.0, slot + (cap * (row >> 3)).astype(jnp.float32))
    column_ids = lax.broadcasted_iota(jnp.int32, (rows, slots), 1).astype(jnp.float32)
    placer[...] = jnp.where(column_ids == target, 1.0, 0.0).astype(jnp.bfloat16)

    for q in range(PIECES):
        sibling_wait(q)
        for load in loads[q]:
            load.wait()
        xq = x[q].reshape(rows, width)
        scaled = (coefficient * xq.astype(jnp.float32)).astype(jnp.bfloat16)
        g, u, h = dot(xq, wg[q]), dot(xq, wu[q]), dot_nt(scaled, wd[q])
        if q == 0:
            gate_acc[...], up_acc[...], gh_acc[...] = g, u, h
        else:
            gate_acc[...] += g
            up_acc[...] += u
            gh_acc[...] += h
        sc_send[q] = dot_tn(placer[...], scaled).astype(jnp.bfloat16)

    sc_copies = []
    for r in range(1, n_dp):
        peer = lax.rem(mine_dp + r, n_dp)
        sc_copies.append(remote(sc_send.at[peer], sc.at[r - 1], sc_s.at[r - 1], sc_r.at[r - 1], dp=peer))
        sc_copies[-1].start()

    gate = gate_acc[...]
    hidden = jnp.where(forward_row, gate * jax.nn.sigmoid(gate) * up_acc[...], 0.0).astype(jnp.bfloat16)
    gate_b = dot(placer[...], pre_ref[0])
    up_b = dot(placer[...], pre_ref[1])
    sg = jax.nn.sigmoid(gate_b)
    grad_hidden = jnp.where(forward_row, 0.0, gh_acc[...])
    grad_gate = (grad_hidden * up_b * sg * (1.0 + gate_b * (1.0 - sg))).astype(jnp.bfloat16)
    grad_up = (grad_hidden * gate_b * sg).astype(jnp.bfloat16)
    scale = jnp.where(forward_row, coefficient, 1.0)

    def output_piece(q):
        value = dot(hidden, wd[q]) + dot_nt(grad_gate, wg[q]) + dot_nt(grad_up, wu[q])
        return (scale * value).reshape(n_chip, 16, width)

    sib_copies = []
    for k in range(2):
        sib_send[k] = output_piece((1 - core) * 2 + k).astype(jnp.bfloat16)
        sib_copies.append(remote(sib_send.at[k], sib_recv.at[k], sib_s.at[k], sib_r.at[k], expert=sib))
        sib_copies[-1].start()
        own[k] = output_piece(core * 2 + k)

    def local(k, d):
        return own[k, d] + sib_recv[k, d].astype(jnp.float32)

    def ring_copy(k, way, s):
        return remote(
            rs_send.at[k, way, s], rs_recv.at[k, way, s], rs_s.at[k, way, s], rs_r.at[k, way, s],
            expert=right if way == 0 else left,
        )

    def send_sum(k, way, s, value):
        rs_send[k, way, s] = value.astype(jnp.bfloat16)
        ring_copy(k, way, s).start()

    for k in range(2):
        sib_copies[k].wait_recv()
        send_sum(k, 0, 0, local(k, lax.rem(z + half, n_chip)))
        send_sum(k, 1, 0, local(k, lax.rem(z + half + 1, n_chip)))

    def pass_on(k, way, s):
        ring_copy(k, way, s).wait_recv()
        d = z + half - 1 - s if way == 0 else z + half + 2 + s
        value = rs_recv[k, way, s].astype(jnp.float32) + local(k, lax.rem(d, n_chip))
        send_sum(k, way, s + 1, value)

    def ring_body(s, carry):
        for k in range(2):
            for way in range(2):
                pass_on(k, way, s)
        return carry

    lax.fori_loop(0, half - 2, ring_body, 0)
    fin_copies = []
    for k in range(2):
        pass_on(k, 0, half - 2)
    for k in range(2):
        ring_copy(k, 1, half - 2).wait_recv()
        ring_copy(k, 0, half - 1).wait_recv()
        value = local(k, z) + rs_recv[k, 1, half - 2].astype(jnp.float32)
        value = value + rs_recv[k, 0, half - 1].astype(jnp.float32)
        start = x[core * 2 + k, pl.ds(z * 2, 2)].reshape(16, width)
        fin_send[k] = (start.astype(jnp.float32) + value).astype(jnp.bfloat16).reshape(2, 8, width)
        for i in range(2):
            q = core * 2 + k
            fin_copies.append(remote(
                fin_send.at[k, i], fin_recv.at[q], fin_s.at[k, i], fin_r.at[q],
                pipe=before, expert=z * 2 + i,
            ))
            fin_copies[-1].start()

    sc[n_dp - 1] = sc_send[mine_dp]
    for copy in hid_copies + sc_copies:
        copy.wait_recv()
    down_out[...] = dot_tn(sc[...].reshape(n_dp * slots, width), hid[...].reshape(n_dp * slots, hid.shape[2]))

    last = pipe == n_pipe - 1
    for q in range(PIECES):
        remote(fin_send.at[0, 0], fin_recv.at[q], fin_s.at[0, 0], fin_r.at[q], expert=sib).wait_recv()
        value = jnp.where(last, 0.0, fin_recv[q].astype(jnp.float32)).astype(jnp.bfloat16)
        acts_out[:, pl.ds(q * width, width)] = value[0:4]
        grads_out[:, pl.ds(q * width, width)] = value[4:8]

    for copy in hid_copies + sc_copies + sib_copies + fin_copies:
        copy.wait_send()
    for k in range(2):
        for way in range(2):
            for s in range(half - way):
                ring_copy(k, way, s).wait_send()
    for q in order:
        for way in range(2):
            for s in range(half - way):
                hop(q, me, right, ag_ring.at[q, way, s]).wait_send()
        for s in range(n_chip):
            hop(q, me, sib, ag_sib.at[q, s]).wait_send()


def shards(
    acts_fwd, ids_fwd, scores_fwd, cot_bwd, ids_bwd, scores_bwd, saved_out, saved_pre, w_gate, w_up, w_down,
):
    n_pipe, n_dev, n_dp = lax.axis_size("pipe"), lax.axis_size("expert"), lax.axis_size("dp")
    model, units = w_gate.shape[1:]
    slots = saved_pre.shape[1]
    width = model // PIECES
    n_chip = n_dev // 2
    half = n_chip // 2
    rows = n_dev * 8
    bf16, f32 = jnp.bfloat16, jnp.float32
    vmem = pl.BlockSpec(memory_space=pltpu.VMEM)
    hbm = pl.BlockSpec(memory_space=pl.ANY)
    dma = pltpu.SemaphoreType.DMA
    scratch = [
        pltpu.VMEM((PIECES, n_dev, 8, width), bf16),
        pltpu.VMEM((n_dev, 8, 128), f32),
        pltpu.VMEM((PIECES, width, units), bf16),
        pltpu.VMEM((PIECES, width, units), bf16),
        pltpu.VMEM((PIECES, units, width), bf16),
        pltpu.VMEM((rows, units), f32),
        pltpu.VMEM((rows, units), f32),
        pltpu.VMEM((rows, units), f32),
        pltpu.VMEM((rows, slots), bf16),
        pltpu.VMEM((n_dp, slots, units), bf16),
        pltpu.VMEM((n_dp, slots, width), bf16),
        pltpu.VMEM((n_dp, slots, width), bf16),
        pltpu.VMEM((2, n_chip, 16, width), bf16),
        pltpu.VMEM((2, n_chip, 16, width), bf16),
        pltpu.VMEM((2, n_chip, 16, width), f32),
        pltpu.VMEM((2, 2, half, 16, width), bf16),
        pltpu.VMEM((2, 2, half, 16, width), bf16),
        pltpu.VMEM((2, 2, 8, width), bf16),
        pltpu.VMEM((PIECES, 8, width), bf16),
        dma((3, PIECES)),
        dma((PIECES + 1, n_dev)),
        dma((PIECES + 1, 2, half)),
        dma((PIECES + 1, n_chip)),
        dma((n_dp - 1,)), dma((n_dp - 1,)), dma((n_dp - 1,)), dma((n_dp - 1,)),
        dma((2,)), dma((2,)),
        dma((2, 2, half)), dma((2, 2, half)),
        dma((2, 2)), dma((PIECES,)),
    ]
    acts_sent, grads_sent, down_grad = pl.pallas_call(
        functools.partial(kernel, n_pipe, n_dev, n_dp, FE // units),
        out_shape=(
            jax.ShapeDtypeStruct(acts_fwd.shape[1:], bf16),
            jax.ShapeDtypeStruct(acts_fwd.shape[1:], bf16),
            jax.ShapeDtypeStruct((width, units), f32),
        ),
        in_specs=[vmem] * 7 + [hbm] * 3,
        out_specs=(vmem, vmem, vmem),
        scratch_shapes=scratch,
        compiler_params=pltpu.CompilerParams(
            collective_id=0, has_side_effects=True, vmem_limit_bytes=56 * 1024 * 1024
        ),
        name="relay_layer",
    )(
        acts_fwd[0], cot_bwd[0], ids_fwd[0].T, scores_fwd[0].T, ids_bwd[0].T, scores_bwd[0].T,
        saved_pre[0].transpose(1, 0, 2),
        w_gate[0].reshape(PIECES, width, units), w_up[0].reshape(PIECES, width, units), w_down[0],
    )
    dots = jnp.einsum("tkd,td->tk", saved_out[0], cot_bwd[0], preferred_element_type=jnp.float32)
    score_grads = score_gradient(scores_bwd[0], dots)
    return (acts_sent[None], grads_sent[None], score_grads[None], down_grad[None])


def solution(mesh):
    token_spec = P("pipe", ("expert", "dp"), None)
    in_specs = (
        token_spec, token_spec, token_spec, token_spec, token_spec, token_spec,
        P("pipe", ("expert", "dp"), None, None),
        P("pipe", "dp", None, "expert"),
        P("pipe", None, "expert"),
        P("pipe", None, "expert"),
        P("pipe", "expert", None),
    )
    out_specs = (token_spec, token_spec, token_spec, P("pipe", "dp", "expert"))
    return jax.shard_map(shards, mesh=mesh, in_specs=in_specs, out_specs=out_specs, check_vma=False)
```

time: 273 us -> 99.7 us (0.37)
  waiting for transfers between devices: 188 us -> 0 us
  Pallas kernels: 0 us -> 88.5 us
  starting transfers between devices: 38.4 us -> 0 us
  between operations: 14.3 us -> 0.65 us
  matrix products: 12.9 us -> 0.96 us
  other arithmetic: 6.65 us -> 2.01 us
  local copies, waits for them, and re-layouts: 10.9 us -> 6.64 us
    all_to_all x4 -> x0, waiting for transfers between devices: 180 us -> none  [the longest x2 90.8 us: expert_round(): lax.all_to_all(buffer, 'expert', split_axis=1, concat_axis=1, tiled=True)]
    pallas_call x0 -> x1, Pallas kernels: none -> 88.5 us  [shards(): pl.pallas_call(functools.partial(kernel, n_pipe, n_dev, n_dp, FE // units...]
    all_to_all x4 -> x0, starting transfers between devices: 33.4 us -> none  [the longest x2 23.7 us: expert_round(): lax.all_to_all(buffer, 'expert', split_axis=1, concat_axis=1, tiled=True)]
    dot_general x10 -> x0, matrix products: 12.6 us -> none  [the longest x1 2.67 us: forward_part(): return jnp.dot(hidden, down_slice, preferred_element_type=jnp.float32)]
    ppermute x2 -> x0, waiting for transfers between devices: 7.6 us -> none  [shifted(): return lax.ppermute(block, axis, route)]
    ppermute x2 -> x0, starting transfers between devices: 4.93 us -> none  [shifted(): return lax.ppermute(block, axis, route)]
    another operation x4 -> x0, local copies, waits for them, and re-layouts: 4.58 us -> none  [the longest x2 2.34 us: expert_round(): jnp.stack(partials, axis=0)]
    unnamed x23 -> x6, local copies, waits for them, and re-layouts: 2.95 us -> 6.54 us
  transfers between devices with their start and end apart: 7 -> 0, of which waited for: 5 -> 0; matrix products, arithmetic and copies ran while one was open for 7% -> 0% of each run, Pallas kernels for 0% -> 0%
where the time goes in v1:
time: 99.7 us; the launch traced here: 98.7 us
  Pallas kernels  88.5 us (89%)
  local copies, waits for them, and re-layouts  6.64 us (7%)
  other arithmetic  2.01 us (2%)
    pallas_call x1, Pallas kernels, shards(): pl.pallas_call(functools.partial(kernel, n_pipe, n_dev, n_dp, FE // units...  88.5 us
    unnamed x6, local copies, waits for them, and re-layouts  6.54 us

profile of v1, /device:TPU:7, one launch (start us, length us, event | category | flops | bytes accessed | tf_op | source)
XLA Modules:
  0.0 98.7 jit_solution(6707466135726547035)
XLA Ops:
  0.6 0.0 copy-start
  0.6 0.7 reduce_sum.18
  1.4 0.1 copy-done
  1.5 1.0 fusion
  2.4 0.1 copy.17
  2.5 0.7 fusion.3
  3.2 0.6 fusion.5
  3.8 1.5 %copy.21 = bf16[1,96,2,256]{3,1,2,0:T(8,128)(2,1)} copy(bf16[1,96,2,256]{3,2,1,0:T(2,128)(2,1)} %param.18) | data formatting | bytes 196608 | tf_op args[7]
  5.4 88.5 %relay_layer.1 = (bf16[4,3584]{1,0:T(4,128)(2,1)}, bf16[4,3584]{1,0:T(4,128)(2,1)}, f32[896,256]{1,0:T(8,128)}) custom-call(bf16[4,3584]{1,0:T(4,128)(2,1)} %bitcast.46, bf16[4,3584]{1,0:T(4,128)(2,1)} %bitcast.48, s32[2,4]{1,0:T(2,128)} %bitcast.52, f32[2,4]{1,0:T(2,128)} %bitcast.53, s32[2,4]{1,0:T(2,128)} %bitcast.54, f32[2,4]{1,0:T(2,128)} %bitcast.51, ...), custom_call_target="tpu_custom_call" | custom-call | tf_op jit(solution)/shard_map/relay_layer/pallas_call | solution.py:351
  93.8 1.4 %copy.25 = bf16[1,4,3584]{2,1,0:T(4,128)(2,1)} copy(bf16[1,4,3584]{2,1,0:T(4,128)(2,1)} %bitcast.50) | data formatting | bytes 57344
  95.2 1.4 %copy.26 = bf16[1,4,3584]{2,1,0:T(4,128)(2,1)} copy(bf16[1,4,3584]{2,1,0:T(4,128)(2,1)} %bitcast.49) | data formatting | bytes 57344
  96.6 2.2 %copy.27 = f32[1,896,256]{2,1,0:T(8,128)} copy(f32[1,896,256]{2,1,0:T(8,128)} %bitcast.44) | data formatting | bytes 1835008
  (1 shorter events, 0.0 us)
Async XLA Ops:
  0.6 0.8 copy-start

commit v2 on v1

v2 whole, which is shorter than its diff:
```python
import functools

import jax
import jax.numpy as jnp
from jax import lax
from jax.experimental import pallas as pl
from jax.experimental.pallas import tpu as pltpu
from jax.sharding import PartitionSpec as P

FE = 2048
ROUTE = (
    (0, None), (1, 0), (-1, 0), (3, 0), (-3, 0), (2, 3), (-2, 4), (4, 3), (-4, 4), (6, 3), (-6, 4),
    (5, 9), (-5, 10), (7, 9), (-7, 10), (8, 9),
)
LANES = 128
MESH = pl.DeviceIdType.MESH
BF16, F32 = jnp.bfloat16, jnp.float32


def column(row):
    n = row.shape[1]
    i = lax.broadcasted_iota(jnp.int32, (n, n), 0)
    j = lax.broadcasted_iota(jnp.int32, (n, n), 1)
    return jnp.sum(jnp.where(i == j, jnp.broadcast_to(row, (n, n)), 0.0), axis=1, keepdims=True)


def routing_rows(ids_t, scores_t, with_slots):
    ids = ids_t.astype(F32)
    weights = 2.5 * scores_t / jnp.sum(scores_t, axis=0, keepdims=True)
    tokens = ids.shape[1]
    lane = lax.broadcasted_iota(jnp.int32, (tokens, LANES), 1)
    lane_expert = (lane & 3).astype(F32)
    weight = jnp.zeros((tokens, LANES), F32)
    hit = jnp.zeros((tokens, LANES), F32)
    for k in range(2):
        match = column(ids[k : k + 1]) == lane_expert
        weight = weight + jnp.where(match, column(weights[k : k + 1]), 0.0)
        hit = hit + jnp.where(match, 1.0, 0.0)
    slots = jnp.full((tokens, LANES), -1.0, F32)
    if with_slots:
        running = jnp.zeros((1, LANES), F32)
        before = []
        for t in range(tokens):
            before.append(running)
            running = running + hit[t : t + 1]
        slots = jnp.where(hit > 0.0, jnp.concatenate(before, axis=0), -1.0)
    high = weight.astype(BF16).astype(F32)
    middle = (weight - high).astype(BF16).astype(F32)
    low = weight - high - middle
    return jnp.where(lane < 4, high, jnp.where(lane < 8, middle, jnp.where(lane < 12, low, slots)))


def dot(a, b):
    return jnp.dot(a, b, preferred_element_type=F32)


def dot_nt(a, b):
    return lax.dot_general(a, b, (((1,), (1,)), ((), ())), preferred_element_type=F32)


def dot_tn(a, b):
    return lax.dot_general(a, b, (((0,), (0,)), ((), ())), preferred_element_type=F32)


def kernel(
    n_pipe, n_dev, n_dp, group,
    acts_hbm, cot_hbm, ids_fwd_hbm, scores_fwd_hbm, ids_bwd_hbm, scores_bwd_hbm,
    pre_hbm, saved_hbm, wg_hbm, wu_hbm, wd_hbm,
    fin_recv, sc, hid, sg_out,
    acts_ref, cot_ref, ids_fwd_ref, scores_fwd_ref, ids_bwd_ref, scores_bwd_ref,
    x, wg, wu, wd, pre_in, saved, pre, coef, scale, placer, scaled, gate_acc, up_acc, gh_acc,
    hid_b, gg_b, gu_b, sc_send, sib_send, sib_recv, own, rs_send, rs_recv, fin_send,
    small_sem, w_sem, in_sem, ag_recv, ag_send, ag_sib, hid_s, hid_r, sc_s, sc_r,
    sib_s, sib_r, rs_s, rs_r, fin_s, fin_r,
):
    n_chip = n_dev // 2
    half = n_chip // 2
    pipe = lax.axis_index("pipe")
    me = lax.axis_index("expert")
    mine_dp = lax.axis_index("dp")
    z, core = lax.div(me, 2), lax.rem(me, 2)
    sib = z * 2 + 1 - core
    before, after = lax.rem(pipe + n_pipe - 1, n_pipe), lax.rem(pipe + 1, n_pipe)
    expert = lax.div(me, group)
    tiles = x.shape[2]
    piece = rs_send.shape[3]
    per_piece = piece // LANES
    per_half = 2 * per_piece
    model = 4 * piece
    slots = pre_in.shape[0]
    cap = slots // n_dev
    batch = half * 16
    bslots = half * 2 * cap

    edges = [(c, ROUTE[c][1]) for c in range(1, n_chip)]

    def chip_at(step):
        return lax.rem(z + step + n_chip, n_chip) * 2 + core

    def remote(src, dst, send_sem, recv_sem, **where):
        return pltpu.make_async_remote_copy(
            src_ref=src, dst_ref=dst, send_sem=send_sem, recv_sem=recv_sem,
            device_id=where, device_id_type=MESH,
        )

    small = [
        pltpu.make_async_copy(source, target, small_sem.at[i])
        for i, (source, target) in enumerate((
            (acts_hbm, acts_ref), (cot_hbm, cot_ref), (ids_fwd_hbm, ids_fwd_ref),
            (scores_fwd_hbm, scores_fwd_ref), (ids_bwd_hbm, ids_bwd_ref), (scores_bwd_hbm, scores_bwd_ref),
        ))
    ]
    for copy in small:
        copy.start()
    barrier = pltpu.get_barrier_semaphore()
    peers = [dict(expert=chip_at(step)) for step in sorted(set(ROUTE[c][0] - ROUTE[p][0] for c, p in edges)
             | set(ROUTE[p][0] - ROUTE[c][0] for c, p in edges))]
    peers += [dict(expert=sib)]
    peers += [dict(dp=lax.rem(mine_dp + r, n_dp)) for r in range(1, n_dp)]
    peers += [dict(pipe=p, expert=d) for p in (before, after) for d in (me, sib)]
    for peer in peers:
        pl.semaphore_signal(barrier, inc=1, device_id=peer, device_id_type=MESH)

    side = [pltpu.make_async_copy(pre_hbm, pre_in, in_sem.at[0]), pltpu.make_async_copy(saved_hbm, saved, in_sem.at[1])]
    loads = []
    for q in range(2):
        cols = pl.ds(q * 2 * piece, 2 * piece)
        loads += [
            pltpu.make_async_copy(wg_hbm.at[q], wg.at[q], w_sem.at[0, q]),
            pltpu.make_async_copy(wu_hbm.at[q], wu.at[q], w_sem.at[1, q]),
            pltpu.make_async_copy(wd_hbm.at[:, cols], wd.at[q], w_sem.at[2, q]),
        ]
    for load in side + loads:
        load.start()

    for copy in small:
        copy.wait()
    x[0, 0, 0] = jnp.concatenate(
        [
            routing_rows(ids_fwd_ref[...], scores_fwd_ref[...], False),
            routing_rows(ids_bwd_ref[...], scores_bwd_ref[...], True),
        ],
        axis=0,
    ).astype(BF16)
    for t in range(tiles - 1):
        part = pl.ds(t * LANES, LANES)
        x[0, 0, 1 + t] = jnp.concatenate([acts_ref[:, part].astype(F32), cot_ref[:, part].astype(F32)], axis=0).astype(BF16)

    pl.semaphore_wait(barrier, len(peers))

    def pass_rows(c):
        p = ROUTE[c][1]
        return remote(
            x.at[p, 0], x.at[c, 0], ag_send.at[c], ag_recv.at[c, 0], expert=chip_at(ROUTE[c][0] - ROUTE[p][0])
        )

    def pass_children(p):
        for c, parent in edges:
            if parent == p:
                pass_rows(c).start()

    def sib_rows(p):
        return remote(x.at[p, 0], x.at[p, 1], ag_sib.at[p], ag_recv.at[p, 1], expert=sib)

    for c in (3, 4, 1, 2):
        pass_rows(c).start()
    sib_rows(0).start()

    def take_rows(*places):
        for p in places:
            pass_rows(p).wait_recv()
            pass_children(p)
            sib_rows(p).start()

    def local_inputs():
        for copy in side:
            copy.wait()
        both = pre_in[...].astype(F32)
        gate_pre, up_pre = both[:, 0, :], both[:, 1, :]
        pre[0], pre[1] = gate_pre.astype(BF16), up_pre.astype(BF16)
        rows = (gate_pre * jax.nn.sigmoid(gate_pre) * up_pre).astype(BF16)
        i = lax.broadcasted_iota(jnp.int32, (slots, slots), 0)
        j = lax.broadcasted_iota(jnp.int32, (slots, slots), 1)
        chip, other, slot = lax.div(i, 2 * cap), lax.rem(lax.div(i, cap), 2), lax.rem(i, cap)
        wanted = origin(chip, other) * cap + slot
        swap = jnp.where(j == wanted, 1.0, 0.0).astype(BF16)
        hid[n_dp - 1] = dot(swap, rows).astype(BF16)

    def origin(p, other):
        step = jnp.zeros_like(p)
        for i in range(n_chip):
            step = jnp.where(p == i, ROUTE[i][0], step)
        chip = lax.rem(z - step + n_chip, n_chip)
        return chip * 2 + jnp.where(other == 0, core, 1 - core)

    def hid_copy(r):
        return remote(
            hid.at[n_dp - 1], hid.at[r - 1], hid_s.at[r - 1], hid_r.at[r - 1], dp=lax.rem(mine_dp + r, n_dp)
        )

    def score_gradients():
        scores = scores_bwd_ref[...]
        token = lax.broadcasted_iota(jnp.int32, scores.shape, 1)
        dots = jnp.zeros(scores.shape, F32)
        for t in range(scores.shape[1]):
            product = saved[t].astype(F32) * cot_ref[t : t + 1, :].astype(F32)
            dots = dots + jnp.where(token == t, jnp.sum(product, axis=1, keepdims=True), 0.0)
        total = jnp.sum(scores, axis=0, keepdims=True)
        sg_out[...] = 2.5 / total * (dots - jnp.sum(dots * scores, axis=0, keepdims=True) / total)

    def tile_rows(b, t):
        return x[b * half : (b + 1) * half, :, t].reshape(batch, LANES)

    def half_rows(b, q):
        return jnp.concatenate([tile_rows(b, 1 + q * per_half + t) for t in range(per_half)], axis=1)

    def is_forward(shape):
        return (lax.broadcasted_iota(jnp.int32, shape, 0) & 7) < 4

    def route(b):
        for p in range(b * half, (b + 1) * half):
            sib_rows(p).wait_recv()
        table = tile_rows(b, 0).astype(F32)
        lane = lax.broadcasted_iota(jnp.int32, (batch, LANES), 1)
        mine = (lane < 12) & ((lane & 3) == expert)
        weight = jnp.sum(jnp.where(mine, table, 0.0), axis=1, keepdims=True)
        slot = jnp.sum(jnp.where(lane == expert + 12, table, 0.0), axis=1, keepdims=True)
        coef[b] = jnp.broadcast_to(weight, (batch, LANES))
        scale[b] = jnp.where(is_forward((batch, LANES)), coef[b], 1.0)
        row = lax.broadcasted_iota(jnp.int32, (batch, 1), 0)
        device = origin(b * half + (row >> 4), (row >> 3) & 1)
        target = jnp.where(slot < 0.0, -1.0, slot + (cap * device).astype(F32))
        ids = lax.broadcasted_iota(jnp.int32, (batch, slots), 1).astype(F32)
        placer[b] = jnp.where(ids == target, 1.0, 0.0).astype(BF16)
        weights = coef[b]
        for t in range(tiles - 1):
            scaled[b, :, t * LANES : (t + 1) * LANES] = (weights * tile_rows(b, 1 + t).astype(F32)).astype(BF16)
        near = jnp.where(slot < 0.0, -1.0, slot + (cap * (row >> 3)).astype(F32))
        near_ids = lax.broadcasted_iota(jnp.int32, (batch, bslots), 1).astype(F32)
        near_placer = jnp.where(near_ids == near, 1.0, 0.0).astype(BF16)
        for q in range(4):
            part = scaled[b, :, q * piece : (q + 1) * piece]
            sc_send[q, b] = dot_tn(near_placer, part).astype(BF16)
        for r in range(1, n_dp):
            sc_copy(r, b).start()

    def sc_copy(r, b):
        peer = lax.rem(mine_dp + r, n_dp)
        return remote(sc_send.at[peer, b], sc.at[r - 1, b], sc_s.at[r - 1, b], sc_r.at[r - 1, b], dp=peer)

    def gate_up(b, q):
        rows = half_rows(b, q)
        g, u = dot(rows, wg[q]), dot(rows, wu[q])
        if q == 0:
            gate_acc[b], up_acc[b] = g, u
        else:
            gate_acc[b] += g
            up_acc[b] += u

    def grad_in(b):
        value = None
        for q in range(2):
            term = dot_nt(scaled[b, :, q * 2 * piece : (q + 1) * 2 * piece], wd[q])
            value = term if value is None else value + term
        gh_acc[b] = value

    def activate(b):
        forward = is_forward((batch, 1))
        gate = gate_acc[b]
        hid_b[b] = jnp.where(forward, gate * jax.nn.sigmoid(gate) * up_acc[b], 0.0).astype(BF16)
        gate_pre = dot(placer[b], pre[0])
        up_pre = dot(placer[b], pre[1])
        sg = jax.nn.sigmoid(gate_pre)
        grad_hidden = jnp.where(forward, 0.0, gh_acc[b])
        gg_b[b] = (grad_hidden * up_pre * sg * (1.0 + gate_pre * (1.0 - sg))).astype(BF16)
        gu_b[b] = (grad_hidden * gate_pre * sg).astype(BF16)

    def output(b, q, k):
        part = slice(k * piece, (k + 1) * piece)
        value = dot(hid_b[b], wd[q, :, part]) + dot_nt(gg_b[b], wg[q, part, :]) + dot_nt(gu_b[b], wu[q, part, :])
        return scale[b][:, 0:1] * value

    def sib_copy(k, b):
        span = pl.ds(b * half, half)
        return remote(sib_send.at[k, span], sib_recv.at[k, span], sib_s.at[k, b], sib_r.at[k, b], expert=sib)

    def output_sib(b, k):
        value = output(b, 1 - core, k).reshape(half, 2, 8, piece).astype(BF16)
        sib_send[k, b * half : (b + 1) * half, 0] = value[:, 1]
        sib_send[k, b * half : (b + 1) * half, 1] = value[:, 0]
        sib_copy(k, b).start()

    def output_own(b, k):
        own[k, b * half : (b + 1) * half] = output(b, core, k).reshape(half, 16, piece)

    def sib_wait(b):
        for k in range(2):
            sib_copy(k, b).wait_recv()

    def pass_sum(c):
        p = ROUTE[c][1]
        return remote(
            rs_send.at[c], rs_recv.at[c], rs_s.at[c], rs_r.at[c], expert=chip_at(ROUTE[p][0] - ROUTE[c][0])
        )

    def total(p, k):
        value = own[k, p] + sib_recv[k, p].astype(F32).reshape(16, piece)
        for c, parent in edges:
            if parent == p:
                value = value + rs_recv[c, k].astype(F32)
        return value

    def give_sums(*places):
        for p in places:
            for c, parent in edges:
                if parent == p:
                    pass_sum(c).wait_recv()
            for k in range(2):
                rs_send[p, k] = total(p, k).astype(BF16)
            pass_sum(p).start()

    local_inputs()
    for r in range(1, n_dp):
        hid_copy(r).start()
    take_rows(1, 2, 3, 4)
    score_gradients()
    take_rows(5, 6, 7, 8, 9, 10)
    route(0)
    take_rows(11, 12, 13, 14, 15)
    for load in loads:
        load.wait()
    gate_up(0, 0)
    gate_up(0, 1)
    route(1)
    gate_up(1, 0)
    gate_up(1, 1)
    grad_in(1)
    activate(1)
    output_sib(1, 0)
    output_sib(1, 1)
    output_own(1, 0)
    output_own(1, 1)
    sib_wait(1)
    give_sums(11, 12, 13, 14, 15)
    grad_in(0)
    activate(0)
    output_sib(0, 0)
    output_sib(0, 1)
    give_sums(9, 10)
    output_own(0, 0)
    output_own(0, 1)
    sib_wait(0)
    give_sums(5, 6, 7, 8, 1, 2)
    give_sums(3, 4)
    for c, parent in edges:
        if parent == 0:
            pass_sum(c).wait_recv()
    fin_copies = []
    for k in range(2):
        first = 1 + core * per_half + k * per_piece
        start = jnp.concatenate([x[0, :, first + t].reshape(16, LANES) for t in range(per_piece)], axis=1)
        fin_send[k] = (start.astype(F32) + total(0, k)).astype(BF16).reshape(2, 8, piece)
        for i in range(2):
            q = core * 2 + k
            fin_copies.append(remote(
                fin_send.at[k, i], fin_recv.at[q], fin_s.at[k, i], fin_r.at[q],
                pipe=before, expert=me if i == 0 else sib,
            ))
            fin_copies[-1].start()

    for b in range(2):
        sc[n_dp - 1, b] = sc_send[mine_dp, b]
    for r in range(1, n_dp):
        hid_copy(r).wait()
        for b in range(2):
            sc_copy(r, b).wait()
    for k in range(2):
        for b in range(2):
            sib_copy(k, b).wait_send()
    for c in range(1, n_chip):
        pass_rows(c).wait_send()
        pass_sum(c).wait_send()
    for p in range(n_chip):
        sib_rows(p).wait_send()
    for copy in fin_copies:
        copy.wait_send()
    for q in range(4):
        remote(fin_send.at[0, 0], fin_recv.at[q], fin_s.at[0, 0], fin_r.at[q], expert=sib).wait_recv()


def finish(n_pipe, fin, sc, hid, sg, acts_out, grads_out, sg_out, down_out):
    last = lax.axis_index("pipe") == n_pipe - 1
    pieces, _, piece = fin.shape
    for q in range(pieces):
        value = jnp.where(last, 0.0, fin[q].astype(F32)).astype(BF16)
        acts_out[:, q * piece : (q + 1) * piece] = value[0:4]
        grads_out[:, q * piece : (q + 1) * piece] = value[4:8]
    sg_out[...] = sg[...]
    rows = hid.shape[0] * hid.shape[1]
    down_out[...] = dot_tn(sc[...].reshape(rows, piece), hid[...].reshape(rows, hid.shape[2]))


def shards(
    acts_fwd, ids_fwd, scores_fwd, cot_bwd, ids_bwd, scores_bwd, saved_out, saved_pre, w_gate, w_up, w_down,
):
    n_pipe, n_dev, n_dp = lax.axis_size("pipe"), lax.axis_size("expert"), lax.axis_size("dp")
    model, units = w_gate.shape[1:]
    slots = saved_pre.shape[1]
    piece = model // 4
    n_chip = n_dev // 2
    half = n_chip // 2
    batch = half * 16
    bslots = slots // 2
    tiles = model // LANES + 1
    vmem = pl.BlockSpec(memory_space=pltpu.VMEM)
    hbm = pl.BlockSpec(memory_space=pltpu.HBM)
    dma = pltpu.SemaphoreType.DMA
    shape = jax.ShapeDtypeStruct
    scratch = [
        pltpu.VMEM(acts_fwd.shape[1:], BF16),
        pltpu.VMEM(acts_fwd.shape[1:], BF16),
        pltpu.VMEM((2, acts_fwd.shape[1]), jnp.int32),
        pltpu.VMEM((2, acts_fwd.shape[1]), F32),
        pltpu.VMEM((2, acts_fwd.shape[1]), jnp.int32),
        pltpu.VMEM((2, acts_fwd.shape[1]), F32),
        pltpu.VMEM((n_chip, 2, tiles, 8, LANES), BF16),
        pltpu.VMEM((2, 2 * piece, units), BF16),
        pltpu.VMEM((2, 2 * piece, units), BF16),
        pltpu.VMEM((2, units, 2 * piece), BF16),
        pltpu.VMEM(saved_pre.shape[1:], BF16),
        pltpu.VMEM(saved_out.shape[1:], BF16),
        pltpu.VMEM((2, slots, units), BF16),
        pltpu.VMEM((2, batch, LANES), F32),
        pltpu.VMEM((2, batch, LANES), F32),
        pltpu.VMEM((2, batch, slots), BF16),
        pltpu.VMEM((2, batch, model), BF16),
        pltpu.VMEM((2, batch, units), F32),
        pltpu.VMEM((2, batch, units), F32),
        pltpu.VMEM((2, batch, units), F32),
        pltpu.VMEM((2, batch, units), BF16),
        pltpu.VMEM((2, batch, units), BF16),
        pltpu.VMEM((2, batch, units), BF16),
        pltpu.VMEM((n_dp, 2, bslots, piece), BF16),
        pltpu.VMEM((2, n_chip, 2, 8, piece), BF16),
        pltpu.VMEM((2, n_chip, 2, 8, piece), BF16),
        pltpu.VMEM((2, n_chip, 16, piece), F32),
        pltpu.VMEM((n_chip, 2, 16, piece), BF16),
        pltpu.VMEM((n_chip, 2, 16, piece), BF16),
        pltpu.VMEM((2, 2, 8, piece), BF16),
        dma((6,)),
        dma((3, 2)),
        dma((2,)),
        dma((n_chip, 2)),
        dma((n_chip,)),
        dma((n_chip,)),
        dma((n_dp - 1,)), dma((n_dp - 1,)), dma((n_dp - 1, 2)), dma((n_dp - 1, 2)),
        dma((2, 2)), dma((2, 2)),
        dma((n_chip,)), dma((n_chip,)),
        dma((2, 2)), dma((4,)),
    ]
    parts = pl.pallas_call(
        functools.partial(kernel, n_pipe, n_dev, n_dp, FE // units),
        out_shape=(
            shape((4, 8, piece), BF16),
            shape((n_dp, 2, bslots, piece), BF16),
            shape((n_dp, slots, units), BF16),
            shape((2, acts_fwd.shape[1]), F32),
        ),
        in_specs=[hbm] * 11,
        out_specs=(vmem,) * 4,
        scratch_shapes=scratch,
        compiler_params=pltpu.CompilerParams(
            collective_id=0, has_side_effects=True, vmem_limit_bytes=36 * 1024 * 1024
        ),
        name="relay_layer",
    )(*map(lambda a: pltpu.with_memory_space_constraint(a, pltpu.HBM), (
        acts_fwd[0], cot_bwd[0], ids_fwd[0].T, scores_fwd[0].T, ids_bwd[0].T, scores_bwd[0].T,
        saved_pre[0], saved_out[0],
        w_gate[0].reshape(2, 2 * piece, units), w_up[0].reshape(2, 2 * piece, units), w_down[0],
    )))
    acts_sent, grads_sent, score_grads, down_grad = pl.pallas_call(
        functools.partial(finish, n_pipe),
        out_shape=(
            shape(acts_fwd.shape[1:], BF16),
            shape(acts_fwd.shape[1:], BF16),
            shape((2, acts_fwd.shape[1]), F32),
            shape((piece, units), F32),
        ),
        in_specs=[vmem] * 4,
        out_specs=(vmem,) * 4,
        compiler_params=pltpu.CompilerParams(vmem_limit_bytes=16 * 1024 * 1024),
        name="relay_finish",
    )(*parts)
    return (acts_sent[None], grads_sent[None], score_grads.T[None], down_grad[None])


def solution(mesh):
    token_spec = P("pipe", ("expert", "dp"), None)
    in_specs = (
        token_spec, token_spec, token_spec, token_spec, token_spec, token_spec,
        P("pipe", ("expert", "dp"), None, None),
        P("pipe", "dp", None, "expert"),
        P("pipe", None, "expert"),
        P("pipe", None, "expert"),
        P("pipe", "expert", None),
    )
    out_specs = (token_spec, token_spec, token_spec, P("pipe", "dp", "expert"))
    return jax.shard_map(shards, mesh=mesh, in_specs=in_specs, out_specs=out_specs, check_vma=False)
```

time: 99.7 us -> 77.7 us (0.78)
  Pallas kernels: 88.5 us -> 76.3 us
  local copies, waits for them, and re-layouts: 6.64 us -> 0 us
  other arithmetic: 2.01 us -> 0 us
    pallas_call x1, Pallas kernels: 88.5 us -> 75 us  [shards(): pl.pallas_call(functools.partial(kernel, n_pipe, n_dev, n_dp, FE // units...]
    unnamed x6 -> x0, local copies, waits for them, and re-layouts: 6.54 us -> none
    reduce_sum x2 -> x0, other arithmetic: 1.43 us -> none  [the longest x1 0.71 us: score_gradient(): score_total = jnp.sum(scores, axis=-1, keepdims=True)]
    pallas_call x0 -> x1, Pallas kernels: none -> 1.37 us  [shards(): pl.pallas_call(functools.partial(finish, n_pipe), out_shape=(shape(acts_f...]
where the time goes in v2:
time: 77.7 us; the launch traced here: 77 us
  Pallas kernels  76.3 us (98%)
    pallas_call x1, Pallas kernels, shards(): pl.pallas_call(functools.partial(kernel, n_pipe, n_dev, n_dp, FE // units...  75 us

profile of v2, /device:TPU:7, one launch (start us, length us, event | category | flops | bytes accessed | tf_op | source)
XLA Modules:
  0.0 77.0 jit_solution(1040864063619150110)
XLA Ops:
  0.6 75.0 %relay_layer.1 = (bf16[4,8,896]{2,1,0:T(8,128)(2,1)S(1)}, bf16[4,2,48,896]{3,2,1,0:T(8,128)(2,1)S(1)}, bf16[4,96,256]{2,1,0:T(8,128)(2,1)S(1)}, f32[2,4]{1,0:T(2,128)S(1)}) custom-call(bf16[4,3584]{1,0:T(4,128)(2,1)} %bitcast.30, bf16[4,3584]{1,0:T(4,128)(2,1)} %bitcast.31, s32[2,4]{1,0:T(2,128)} %bitcast.32, f32[2,4]{1,0:T(2,128)} %bitcast.33, ...), custom_call_target="tpu_custom_call" | custom-call | tf_op jit(solution)/shard_map/relay_layer/pallas_call | solution.py:461
  75.6 1.4 %relay_finish.1 = (bf16[4,3584]{1,0:T(4,128)(2,1)}, bf16[4,3584]{1,0:T(4,128)(2,1)}, f32[2,4]{1,0:T(2,128)}, f32[896,256]{1,0:T(8,128)}) custom-call(bf16[4,8,896]{2,1,0:T(8,128)(2,1)S(1)} %get-tuple-element.12.fin, bf16[4,2,48,896]{3,2,1,0:T(8,128)(2,1)S(1)} %get-tuple-element.13.sc, bf16[4,96,256]{2,1,0:T(8,128)(2,1)S(1)} %get-tuple-element.14.hid, ...), custom_call_target="tpu_custom_call" | custom-call | tf_op jit(solution)/shard_map/relay_finish/pallas_call | solution.py:481

commit v3 on v2

--- a/solution.py
+++ b/solution.py
@@ -280,22 +280,26 @@
         value = dot(hid_b[b], wd[q, :, part]) + dot_nt(gg_b[b], wg[q, part, :]) + dot_nt(gu_b[b], wu[q, part, :])
         return scale[b][:, 0:1] * value
 
-    def sib_copy(k, b):
-        span = pl.ds(b * half, half)
-        return remote(sib_send.at[k, span], sib_recv.at[k, span], sib_s.at[k, b], sib_r.at[k, b], expert=sib)
+    spans = [pl.ds(0, half), pl.ds(half, 3), pl.ds(half + 3, half - 3)]
+
+    def sib_copy(k, i):
+        return remote(
+            sib_send.at[k, spans[i]], sib_recv.at[k, spans[i]], sib_s.at[k, i], sib_r.at[k, i], expert=sib
+        )
 
     def output_sib(b, k):
         value = output(b, 1 - core, k).reshape(half, 2, 8, piece).astype(BF16)
         sib_send[k, b * half : (b + 1) * half, 0] = value[:, 1]
         sib_send[k, b * half : (b + 1) * half, 1] = value[:, 0]
-        sib_copy(k, b).start()
+        for i in (2, 1) if b == 1 else (0,):
+            sib_copy(k, i).start()
 
     def output_own(b, k):
         own[k, b * half : (b + 1) * half] = output(b, core, k).reshape(half, 16, piece)
 
-    def sib_wait(b):
+    def sib_wait(i):
         for k in range(2):
-            sib_copy(k, b).wait_recv()
+            sib_copy(k, i).wait_recv()
 
     def pass_sum(c):
         p = ROUTE[c][1]
@@ -340,12 +344,13 @@
     output_sib(1, 1)
     output_own(1, 0)
     output_own(1, 1)
-    sib_wait(1)
-    give_sums(11, 12, 13, 14, 15)
+    sib_wait(2)
+    give_sums(15, 13, 14, 11, 12)
     grad_in(0)
     activate(0)
     output_sib(0, 0)
     output_sib(0, 1)
+    sib_wait(1)
     give_sums(9, 10)
     output_own(0, 0)
     output_own(0, 1)
@@ -375,8 +380,8 @@
         for b in range(2):
             sc_copy(r, b).wait()
     for k in range(2):
-        for b in range(2):
-            sib_copy(k, b).wait_send()
+        for i in range(len(spans)):
+            sib_copy(k, i).wait_send()
     for c in range(1, n_chip):
         pass_rows(c).wait_send()
         pass_sum(c).wait_send()
@@ -454,7 +459,7 @@
         dma((n_chip,)),
         dma((n_chip,)),
         dma((n_dp - 1,)), dma((n_dp - 1,)), dma((n_dp - 1, 2)), dma((n_dp - 1, 2)),
-        dma((2, 2)), dma((2, 2)),
+        dma((2, 3)), dma((2, 3)),
         dma((n_chip,)), dma((n_chip,)),
         dma((2, 2)), dma((4,)),
     ]

time: 77.7 us -> 77.9 us (level)
  Pallas kernels: 76.3 us -> 77.1 us
    pallas_call x1, Pallas kernels: 75 us -> 75.8 us  [shards(): pl.pallas_call(functools.partial(kernel, n_pipe, n_dev, n_dp, FE // units...]
where the time goes in v3:
time: 77.9 us; the launch traced here: 77.8 us
  Pallas kernels  77.1 us (99%)
    pallas_call x1, Pallas kernels, shards(): pl.pallas_call(functools.partial(kernel, n_pipe, n_dev, n_dp, FE // units...  75.8 us

profile of v3, /device:TPU:7, one launch (start us, length us, event | category | flops | bytes accessed | tf_op | source)
XLA Modules:
  0.0 77.8 jit_solution(3448466371314897624)
XLA Ops:
  0.6 75.8 %relay_layer.1 = (bf16[4,8,896]{2,1,0:T(8,128)(2,1)S(1)}, bf16[4,2,48,896]{3,2,1,0:T(8,128)(2,1)S(1)}, bf16[4,96,256]{2,1,0:T(8,128)(2,1)S(1)}, f32[2,4]{1,0:T(2,128)S(1)}) custom-call(bf16[4,3584]{1,0:T(4,128)(2,1)} %bitcast.30, bf16[4,3584]{1,0:T(4,128)(2,1)} %bitcast.31, s32[2,4]{1,0:T(2,128)} %bitcast.32, f32[2,4]{1,0:T(2,128)} %bitcast.33, ...), custom_call_target="tpu_custom_call" | custom-call | tf_op jit(solution)/shard_map/relay_layer/pallas_call | solution.py:466
  76.4 1.4 %relay_finish.1 = (bf16[4,3584]{1,0:T(4,128)(2,1)}, bf16[4,3584]{1,0:T(4,128)(2,1)}, f32[2,4]{1,0:T(2,128)}, f32[896,256]{1,0:T(8,128)}) custom-call(bf16[4,8,896]{2,1,0:T(8,128)(2,1)S(1)} %get-tuple-element.12.fin, bf16[4,2,48,896]{3,2,1,0:T(8,128)(2,1)S(1)} %get-tuple-element.13.sc, bf16[4,96,256]{2,1,0:T(8,128)(2,1)S(1)} %get-tuple-element.14.hid, ...), custom_call_target="tpu_custom_call" | custom-call | tf_op jit(solution)/shard_map/relay_finish/pallas_call | solution.py:486
